TPU v7x, 32 devices: a whole 2x2x4 slice. The times are simulated.
32 devices in a mesh: dp: 8 (over y, x, core), tensor: 4 (over z).
Axes of the slice: x: 2, y: 2, z: 4, core: 2. Of those that a mesh axis runs over, the one named last changes fastest.
Arguments:
- tokens: bfloat16 [8192, 2048], P(('dp', 'tensor')), may hold values from -6 to 6
- seq_start: int32 [8192], P('dp'), may hold values from 0 to 8191, as said below
- proj_weight: bfloat16 [2048, 3, 2048], P('dp', None, 'tensor'), may hold values from -0.125 to 0.125
- proj_bias: bfloat16 [3, 8, 256], P(None, 'tensor', 'dp'), may hold values from -3 to 3
- out_weight: bfloat16 [2048, 2048], P('tensor', 'dp'), may hold values from -1.5 to 1.5
- up_weight: bfloat16 [2048, 8192], P('dp', 'tensor'), may hold values from -0.125 to 0.125
- up_bias: bfloat16 [4, 2048], P('tensor', 'dp'), may hold values from -3 to 3
- down_weight: bfloat16 [8192, 2048], P('tensor', 'dp'), may hold values from -0.0625 to 0.0625
- norm_gains: bfloat16 [2, 2048], P(None, ('dp', 'tensor')), may hold values from 0.099609375 to 1.8984375
- biases: bfloat16 [4, 2048], P(None, ('dp', 'tensor')), may hold values from -3 to 3
- cotangent: bfloat16 [8192, 2048], P(('dp', 'tensor')), may hold values from -6 to 6
Outputs:
- output: bfloat16 [8192, 2048], P(('dp', 'tensor'))
- input_grad: float32 [8192, 2048], P(('dp', 'tensor'))
- proj_grad: float32 [2048, 3, 2048], P('dp', None, 'tensor')
- proj_bias_grad: float32 [3, 8, 256], P(None, 'tensor', 'dp')
- out_grad: float32 [2048, 2048], P('tensor', 'dp')
- up_grad: float32 [2048, 8192], P('dp', 'tensor')
- up_bias_grad: float32 [4, 2048], P('tensor', 'dp')
- down_grad: float32 [8192, 2048], P('tensor', 'dp')
- gains_grad: float32 [2, 2048], P(None, ('dp', 'tensor'))
- biases_grad: float32 [4, 2048], P(None, ('dp', 'tensor'))
Inputs may be any that keep to these rules, and one draw needn't show every extreme that they name: seq_start never falls along the tokens, is at most the token's own index, and every sequence lies inside one aligned block of 1024 tokens (the tokens of one index of dp); some block other than the last holds a single sequence of 1024 tokens, the others hold sequences of uneven lengths, and the last token begins a sequence of its own.
All inputs are finite; a program needn't handle non-finite values.
Results may differ from a plain program's by a relative error of at most 0.012.
Values may be sent and summed in bfloat16 or wider, within the bound.
No kernel may reach another device: no remote copies, remote signals or barrier semaphores. Data moves between devices by JAX's collectives and lax.ppermute only.
A program may use at most 192 MiB of HBM per device.

v0:
```python
import jax
import jax.numpy as jnp
from jax import lax
from jax.sharding import PartitionSpec as P

ROT = 64
EPSILON = 1e-05
ROTARY_BASE = 10000.0


def layer_norm(values, gain_row, shift_row):
    centered = values - jnp.mean(values, axis=-1, keepdims=True)
    spread = jnp.mean(centered * centered, axis=-1, keepdims=True)
    return centered * lax.rsqrt(spread + EPSILON) * gain_row + shift_row


def both_norms(values, gain_rows, shift_rows):
    return (
        layer_norm(values, gain_rows[0], shift_rows[0]),
        layer_norm(values, gain_rows[1], shift_rows[1]),
    )


def gelu_exact(inputs):
    return jax.nn.gelu(inputs, approximate=False)


def rotate(values, positions, turn_sign):
    half_rot = ROT // 2
    frequency = ROTARY_BASE ** (-(jnp.arange(half_rot, dtype=jnp.float32) * 2.0) / ROT)
    angles = positions.astype(jnp.float32)[:, None] * frequency[None, :]
    cosine = jnp.cos(angles)[:, None, :]
    sine_term = turn_sign * jnp.sin(angles)[:, None, :]
    first_half = values[..., :half_rot]
    second_half = values[..., half_rot:ROT]
    return jnp.concatenate(
        [
            first_half * cosine - second_half * sine_term,
            second_half * cosine + first_half * sine_term,
            values[..., ROT:],
        ],
        axis=-1,
    )


def masked_scores(query_block, key_rows, starts, block_start, block_rows):
    row_count = key_rows.shape[0]
    score_scale = key_rows.shape[-1] ** (-0.5)
    key_index = jnp.arange(row_count, dtype=jnp.int32)
    query_begin = lax.dynamic_slice_in_dim(starts, block_start, block_rows, 0)
    query_index = block_start + jnp.arange(block_rows, dtype=jnp.int32)
    scores = (
        jnp.einsum("qhe,khe->hqk", query_block, key_rows, preferred_element_type=jnp.float32)
        * score_scale
    )
    allowed = (query_begin[:, None] == starts[None, :]) & (
        key_index[None, :] <= query_index[:, None]
    )
    return jnp.where(allowed[None], scores, -1e30)


def attention_forward(queries, key_rows, value_rows, starts, block_rows):
    row_count = queries.shape[0]

    def one_block(block_start):
        query_block = lax.dynamic_slice_in_dim(queries, block_start, block_rows, 0)
        scores = masked_scores(query_block, key_rows, starts, block_start, block_rows)
        row_max = jnp.max(scores, axis=-1, keepdims=True)
        powers = jnp.exp(scores - row_max)
        row_total = jnp.sum(powers, axis=-1, keepdims=True)
        weights = (powers / row_total).astype(jnp.bfloat16)
        attended = jnp.einsum(
            "hqk,khe->qhe", weights, value_rows, preferred_element_type=jnp.float32
        )
        return (attended, (row_max + jnp.log(row_total))[..., 0])

    block_starts = jnp.arange(row_count // block_rows, dtype=jnp.int32) * block_rows
    attended, log_total = lax.map(one_block, block_starts)
    return (attended.reshape(queries.shape), log_total)


def attention_backward(queries, key_rows, value_rows, starts, log_total, grad_attended, block_rows):
    row_count = queries.shape[0]
    score_scale = queries.shape[-1] ** (-0.5)

    def one_block(accumulated, pieces):
        block_start, block_total = pieces
        grad_keys, grad_values = accumulated
        query_block = lax.dynamic_slice_in_dim(queries, block_start, block_rows, 0)
        grad_block = lax.dynamic_slice_in_dim(grad_attended, block_start, block_rows, 0)
        scores = masked_scores(query_block, key_rows, starts, block_start, block_rows)
        probs = jnp.exp(scores - block_total[..., None])
        grad_values = grad_values + jnp.einsum(
            "hqk,qhe->khe",
            probs.astype(jnp.bfloat16),
            grad_block,
            preferred_element_type=jnp.float32,
        )
        grad_probs = jnp.einsum(
            "qhe,khe->hqk", grad_block, value_rows, preferred_element_type=jnp.float32
        )
        inner_sum = jnp.sum(probs * grad_probs, axis=-1, keepdims=True)
        grad_scores = (probs * (grad_probs - inner_sum)).astype(jnp.bfloat16)
        grad_query = (
            jnp.einsum("hqk,khe->qhe", grad_scores, key_rows, preferred_element_type=jnp.float32)
            * score_scale
        )
        grad_keys = (
            grad_keys
            + jnp.einsum(
                "hqk,qhe->khe", grad_scores, query_block, preferred_element_type=jnp.float32
            )
            * score_scale
        )
        return ((grad_keys, grad_values), grad_query)

    block_starts = jnp.arange(row_count // block_rows, dtype=jnp.int32) * block_rows
    zeros_like_keys = jnp.zeros(queries.shape, jnp.float32)
    (grad_keys, grad_values), grad_queries = lax.scan(
        one_block, (zeros_like_keys, zeros_like_keys), (block_starts, log_total)
    )
    return (grad_queries.reshape(queries.shape), grad_keys, grad_values)


def shards(
    tokens,
    seq_start,
    proj_weight,
    proj_bias,
    out_weight,
    up_weight,
    up_bias,
    down_weight,
    norm_gains,
    biases,
    cotangent,
):
    local_rows = tokens.shape[0]
    row_count = local_rows * lax.axis_size("tensor")
    block_rows = min(512, row_count)
    dp_index = lax.axis_index("dp")
    gathered = (
        lax.all_gather(proj_weight, "dp", axis=0, tiled=True),
        lax.all_gather(proj_bias, "dp", axis=2, tiled=True),
        lax.all_gather(out_weight, "dp", axis=1, tiled=True),
        lax.all_gather(up_weight, "dp", axis=0, tiled=True),
        lax.all_gather(up_bias, "dp", axis=1, tiled=True),
        lax.all_gather(down_weight, "dp", axis=1, tiled=True),
    )
    joined_weight, joined_bias, mix_weight, hidden_weight, hidden_bias, back_weight = gathered
    gain_rows, shift_rows = (
        lax.all_gather(norm_gains, ("dp", "tensor"), axis=1, tiled=True),
        lax.all_gather(biases, ("dp", "tensor"), axis=1, tiled=True),
    )
    gain_rows = gain_rows.astype(jnp.float32)
    shift_rows = shift_rows.astype(jnp.float32)
    local_f = tokens.astype(jnp.float32)
    first_local, second_local = both_norms(local_f, gain_rows, shift_rows)
    first_rows, second_rows = (
        lax.all_gather(first_local.astype(jnp.bfloat16), "tensor", axis=0, tiled=True),
        lax.all_gather(second_local.astype(jnp.bfloat16), "tensor", axis=0, tiled=True),
    )
    heads_here = joined_bias.shape[1]
    head_size = joined_bias.shape[2]
    local_width = heads_here * head_size
    projected = jnp.einsum(
        "nd,dch->nch", first_rows, joined_weight, preferred_element_type=jnp.float32
    ) + joined_bias.astype(jnp.float32).reshape(3, local_width)
    positions = dp_index * row_count + jnp.arange(row_count, dtype=jnp.int32) - seq_start
    queries = rotate(
        projected[:, 0].reshape(row_count, heads_here, head_size), positions, 1.0
    ).astype(jnp.bfloat16)
    key_rows = rotate(
        projected[:, 1].reshape(row_count, heads_here, head_size), positions, 1.0
    ).astype(jnp.bfloat16)
    value_rows = projected[:, 2].reshape(row_count, heads_here, head_size).astype(jnp.bfloat16)
    attended, log_total = attention_forward(queries, key_rows, value_rows, seq_start, block_rows)
    attended = attended.reshape(row_count, local_width).astype(jnp.bfloat16)
    hidden = jnp.dot(
        second_rows, hidden_weight, preferred_element_type=jnp.float32
    ) + hidden_bias.astype(jnp.float32)
    activated = gelu_exact(hidden).astype(jnp.bfloat16)
    attn_part = jnp.dot(attended, mix_weight, preferred_element_type=jnp.float32)
    branches = lax.psum_scatter(
        attn_part + jnp.dot(activated, back_weight, preferred_element_type=jnp.float32),
        "tensor",
        scatter_dimension=0,
        tiled=True,
    )
    output = (local_f + branches + shift_rows[2] + shift_rows[3]).astype(jnp.bfloat16)
    grad_rows = lax.all_gather(cotangent, "tensor", axis=0, tiled=True)
    regathered = (
        lax.all_gather(proj_weight, "dp", axis=0, tiled=True),
        lax.all_gather(proj_bias, "dp", axis=2, tiled=True),
        lax.all_gather(out_weight, "dp", axis=1, tiled=True),
        lax.all_gather(up_weight, "dp", axis=0, tiled=True),
        lax.all_gather(up_bias, "dp", axis=1, tiled=True),
        lax.all_gather(down_weight, "dp", axis=1, tiled=True),
    )
    joined_again, _, mix_again, hidden_again, _, back_again = regathered
    grad_active = jnp.einsum("nd,fd->nf", grad_rows, back_again, preferred_element_type=jnp.float32)
    down_term = jnp.einsum("nf,nd->fd", activated, grad_rows, preferred_element_type=jnp.float32)
    _, gelu_back = jax.vjp(gelu_exact, hidden)
    grad_hidden = gelu_back(grad_active)[0].astype(jnp.bfloat16)
    up_term = jnp.einsum("nd,nf->df", second_rows, grad_hidden, preferred_element_type=jnp.float32)
    up_bias_term = jnp.sum(grad_hidden, axis=0, keepdims=True, dtype=jnp.float32)
    grad_second = jnp.einsum(
        "nf,df->nd", grad_hidden, hidden_again, preferred_element_type=jnp.float32
    )
    grad_attended = jnp.einsum(
        "nd,ed->ne", grad_rows, mix_again, preferred_element_type=jnp.float32
    ).astype(jnp.bfloat16)
    mix_term = jnp.einsum("ne,nd->ed", attended, grad_rows, preferred_element_type=jnp.float32)
    query_back, key_back, value_back = attention_backward(
        queries,
        key_rows,
        value_rows,
        seq_start,
        log_total,
        grad_attended.reshape(row_count, heads_here, head_size),
        block_rows,
    )
    query_back = rotate(query_back, positions, -1.0).reshape(row_count, local_width)
    key_back = rotate(key_back, positions, -1.0).reshape(row_count, local_width)
    grad_projected = jnp.stack(
        [query_back, key_back, value_back.reshape(row_count, local_width)], axis=1
    ).astype(jnp.bfloat16)
    joined_term = jnp.einsum(
        "nd,nch->dch", first_rows, grad_projected, preferred_element_type=jnp.float32
    )
    joined_bias_term = jnp.sum(grad_projected, axis=0, dtype=jnp.float32).reshape(
        3, heads_here, head_size
    )
    grad_first = jnp.einsum(
        "nch,dch->nd", grad_projected, joined_again, preferred_element_type=jnp.float32
    )
    grad_local = cotangent.astype(jnp.float32)
    first_sum, second_sum = (
        lax.psum_scatter(
            grad_first.astype(jnp.bfloat16), "tensor", scatter_dimension=0, tiled=True
        ).astype(jnp.float32),
        lax.psum_scatter(
            grad_second.astype(jnp.bfloat16), "tensor", scatter_dimension=0, tiled=True
        ).astype(jnp.float32),
    )
    _, norm_back = jax.vjp(both_norms, local_f, gain_rows, shift_rows)
    grad_norm_in, gain_term, shift_term = norm_back((first_sum, second_sum))
    input_grad = grad_local + grad_norm_in
    column_sums = jnp.sum(grad_local, axis=0)
    shift_term = jnp.concatenate([shift_term[:2], jnp.stack([column_sums, column_sums])], axis=0)
    gains_grad, biases_grad = (
        lax.psum_scatter(gain_term, ("dp", "tensor"), scatter_dimension=1, tiled=True),
        lax.psum_scatter(shift_term, ("dp", "tensor"), scatter_dimension=1, tiled=True),
    )
    summed = (
        lax.psum_scatter(joined_term, "dp", scatter_dimension=0, tiled=True),
        lax.psum_scatter(joined_bias_term, "dp", scatter_dimension=2, tiled=True),
        lax.psum_scatter(mix_term, "dp", scatter_dimension=1, tiled=True),
        lax.psum_scatter(up_term, "dp", scatter_dimension=0, tiled=True),
        lax.psum_scatter(up_bias_term, "dp", scatter_dimension=1, tiled=True),
        lax.psum_scatter(down_term, "dp", scatter_dimension=1, tiled=True),
    )
    return (
        output,
        input_grad,
        summed[0],
        summed[1],
        summed[2],
        summed[3],
        summed[4],
        summed[5],
        gains_grad,
        biases_grad,
    )


def solution(mesh):
    in_specs = (
        P(("dp", "tensor"), None),
        P("dp"),
        P("dp", None, "tensor"),
        P(None, "tensor", "dp"),
        P("tensor", "dp"),
        P("dp", "tensor"),
        P("tensor", "dp"),
        P("tensor", "dp"),
        P(None, ("dp", "tensor")),
        P(None, ("dp", "tensor")),
        P(("dp", "tensor"), None),
    )
    out_specs = (
        P(("dp", "tensor"), None),
        P(("dp", "tensor"), None),
        P("dp", None, "tensor"),
        P(None, "tensor", "dp"),
        P("tensor", "dp"),
        P("dp", "tensor"),
        P("tensor", "dp"),
        P("tensor", "dp"),
        P(None, ("dp", "tensor")),
        P(None, ("dp", "tensor")),
    )
    return jax.shard_map(shards, mesh=mesh, in_specs=in_specs, out_specs=out_specs, check_vma=False)
```

profile of v0, /device:TPU:0, one launch (start us, length us, event | category | flops | bytes accessed | tf_op | source)
XLA Modules:
  0.0 1526.1 jit_solution(3073304048536600505)
XLA Ops:
  8.7 71.2 %all-gather = bf16[32,64,2]{1,2,0:T(2,128)(2,1)S(1)} all-gather(bf16[1,64,2]{1,2,0:T(2,128)(2,1)} %bitcast.182), channel_id=1, replica_groups=mesh['dp'=8,'tensor'=4] {'dp','tensor'}, dimensions={0}, use_global_device_ids=true | all-gather | bytes 8448 | tf_op jit(solution)/shard_map/all_gather | solution.py:152
  80.0 66.0 %all-gather.1 = bf16[32,64,4]{1,2,0:T(4,128)(2,1)S(1)} all-gather(bf16[1,64,4]{1,2,0:T(4,128)(2,1)} %bitcast.181), channel_id=1, replica_groups=mesh['dp'=8,'tensor'=4] {'dp','tensor'}, dimensions={0}, use_global_device_ids=true | all-gather | bytes 16896 | tf_op jit(solution)/shard_map/all_gather | solution.py:153
  183.8 47.5 %all-gather.10.cloned.1.call-done = bf16[1024,2048]{1,0:T(8,128)(2,1)} async-done(((bf16[256,2048]{1,0:T(8,128)(2,1)}), bf16[1024,2048]{1,0:T(8,128)(2,1)}) %all-gather.10.cloned.1.call-update) | async-done | bytes 4194320 | tf_op jit(solution)/shard_map/all_gather | solution.py:160
  231.3 47.4 %all-gather.12.cloned.1.call-done = bf16[2048,3,512]{0,2,1:T(8,128)(2,1)} async-done(((bf16[256,3,512]{0,2,1:T(8,128)(2,1)}), bf16[2048,3,512]{0,2,1:T(8,128)(2,1)}) %all-gather.12.cloned.1.call-update) | async-done | bytes 6291472 | tf_op jit(solution)/shard_map/all_gather | solution.py:143
  324.7 20.5 %while.27 = (s32[]{:T(128)}, bf16[2,512,2,256]{3,1,2,0:T(8,128)(2,1)}, f32[2,2,512]{2,1,0:T(2,128)S(1)}, s32[2]{0:T(128)S(1)}, s32[1024]{0:T(1024)S(1)}, /*index...) while((s32[]{:T(128)}, ...), condition=%wide.region_5.6_spmd, body=%wide.region_2.5_spmd.sunk | while | flops 1087897088 | bytes 26786032 | solution.py:78
  345.2 30.7 %while.28 = (s32[]{:T(128)}, f32[1024,2,256]{0,2,1:T(8,128)S(1)}, f32[1024,2,256]{0,2,1:T(8,128)}, f32[2,512,2,256]{3,1,0,2:T(8,128)}, s32[2]{0:T(128)S(1)}, /*i...) while((s32[]{:T(128)}, f32[1024,2,256]{0,2,1:T(8,128)S(1)}, ...), condition=%wide.region_12.13_spmd.clone, body=%wide.region_10.12_spmd.clone.sunk | while | flops 2704539136 | bytes 94415280 | solution.py:119
  394.5 11.4 bitcast_convert_fusion
  416.0 14.8 fusion.78
  430.8 42.9 %all-gather.20.cloned.1.call-done = bf16[2048,2048]{1,0:T(8,128)(2,1)} async-done(((bf16[2048,256]{1,0:T(8,128)(2,1)}), bf16[2048,2048]{1,0:T(8,128)(2,1)}) %all-gather.20.cloned.1.call-update) | async-done | bytes 8388624 | tf_op jit(solution)/shard_map/all_gather | solution.py:148
  473.8 33.0 %convert_reduce_fusion = (f32[2048]{0:T(1024)S(1)}, bf16[1024,2048]{1,0:T(8,128)(2,1)S(1)}, f32[1024,2048]{1,0:T(8,128)}) fusion(f32[1024,2048]{1,0:T(8,128)} %fusion.78, f32[2048]{0:T(1024)S(1)} %bitcast.166, bf16[1024,2048]{1,0:T(8,128)(2,1)} %all-gather.22.cloned.1.call-done, bf16[2048,2048]{1,0:T(8,128)(2,1)} %all-gather.20.cloned.1.call-done), kind=kOutput, calls=%fused_computation.50 | convolution fusion | flops 8747218944 | bytes 33570816 | tf_op jit(solution)/shard_map/nd,fd->nf/dot_general | solution.py:201
  508.7 10.9 convolution_convert_fusion
  532.2 12.7 fusion.79
  556.6 75.9 %reduce-scatter.22.cloned.1.call-done = bf16[256,2048]{1,0:T(8,128)(2,1)} async-done(((bf16[1024,2048]{1,0:T(8,128)(2,1)}), bf16[256,2048]{1,0:T(8,128)(2,1)}) %reduce-scatter.22.cloned.1.call-update) | async-done | bytes 1048592 | tf_op jit(solution)/shard_map/reduce_scatter | solution.py:242
  640.1 139.7 %reduce-scatter.20.cloned.1.call-done = f32[256,2048]{1,0:T(8,128)} async-done(((f32[1024,2048]{1,0:T(8,128)}), f32[256,2048]{1,0:T(8,128)}) %reduce-scatter.20.cloned.1.call-update) | async-done | bytes 2097168 | tf_op jit(solution)/shard_map/reduce_scatter | solution.py:184
  795.0 11.6 fusion.41
  806.7 15.3 %fusion.82 = f32[2048,2048]{1,0:T(8,128)} fusion(bf16[1024,2048]{1,0:T(8,128)(2,1)} %multiply_convert_fusion.1, bf16[1024,2048]{1,0:T(8,128)(2,1)} %all-gather.22.cloned.1.call-done), kind=kOutput, calls=%fused_computation.157 | convolution fusion | flops 8589934592 | bytes 25165824 | tf_op jit(solution)/shard_map/nf,nd->fd/dot_general | solution.py:202
  822.4 15.3 %fusion.81 = f32[2048,2048]{1,0:T(8,128)} fusion(bf16[1024,2048]{1,0:T(8,128)(2,1)} %all-gather.16.cloned.1.call-done, bf16[1024,2048]{1,0:T(8,128)(2,1)} %copy-done.45), kind=kOutput, calls=%fused_computation.156 | convolution fusion | flops 8589934592 | bytes 25165824 | tf_op jit(solution)/shard_map/nd,nf->df/dot_general | solution.py:205
  839.3 16.8 %reduce-scatter.36.cloned.1.call-done = f32[256,1]{1,0:T(8,128)} async-done(((f32[2048,1]{1,0:T(8,128)}), f32[256,1]{1,0:T(8,128)}) %reduce-scatter.36.cloned.1.call-update) | async-done | bytes 1040
  857.6 138.1 %reduce-scatter.38.cloned.1.call-done = f32[64,2]{1,0:T(8,128)} async-done(((f32[2048,2]{1,0:T(8,128)}), f32[64,2]{1,0:T(8,128)}) %reduce-scatter.38.cloned.1.call-update) | async-done | bytes 528
  997.1 134.3 %reduce-scatter.40.cloned.1.call-done = f32[64,4]{1,0:T(8,128)} async-done(((f32[2048,4]{1,0:T(8,128)}), f32[64,4]{1,0:T(8,128)}) %reduce-scatter.40.cloned.1.call-update) | async-done | bytes 1040
  1132.9 49.8 %reduce-scatter.28.cloned.1.call-done = f32[512,256]{1,0:T(8,128)} async-done(((f32[512,2048]{1,0:T(8,128)}), f32[512,256]{1,0:T(8,128)}) %reduce-scatter.28.cloned.1.call-update) | async-done | bytes 524304 | tf_op jit(solution)/shard_map/reduce_scatter | solution.py:258
  1182.7 96.0 %reduce-scatter.26.cloned.1.call-done = f32[256,3,512]{2,0,1:T(8,128)} async-done(((f32[2048,3,512]{2,0,1:T(8,128)}), f32[256,3,512]{2,0,1:T(8,128)}) %reduce-scatter.26.cloned.1.call-update) | async-done | bytes 1572880 | tf_op jit(solution)/shard_map/reduce_scatter | solution.py:256
  1278.8 120.0 %reduce-scatter.32.cloned.1.call-done = f32[2048,256]{1,0:T(8,128)} async-done(((f32[2048,2048]{1,0:T(8,128)}), f32[2048,256]{1,0:T(8,128)}) %reduce-scatter.32.cloned.1.call-update) | async-done | bytes 2097168 | tf_op jit(solution)/shard_map/reduce_scatter | solution.py:261
  1398.8 120.2 %reduce-scatter.30.cloned.1.call-done = f32[256,2048]{1,0:T(8,128)} async-done(((f32[2048,2048]{1,0:T(8,128)}), f32[256,2048]{1,0:T(8,128)}) %reduce-scatter.30.cloned.1.call-update) | async-done | bytes 2097168 | tf_op jit(solution)/shard_map/reduce_scatter | solution.py:259
  (275 shorter events, 211.5 us)
Async XLA Ops:
  7.2 143.3 %copy-start.1 = (bf16[256,2048]{1,0:T(8,128)(2,1)S(1)}, bf16[256,2048]{1,0:T(8,128)(2,1)}, u32[]{:S(2)}) copy-start(bf16[256,2048]{1,0:T(8,128)(2,1)} %param.15) | copy-start | bytes 3145732
  7.2 145.4 %copy-start.28 = (bf16[256,3,512]{2,0,1:T(8,128)(2,1)S(1)}, bf16[256,3,512]{2,0,1:T(8,128)(2,1)}, u32[]{:S(2)}) copy-start(bf16[256,3,512]{2,0,1:T(8,128)(2,1)} %param.17) | copy-start | bytes 2359300
  7.2 170.4 %all-gather.14.cloned.1.call-start = ((), (), s32[]{:S(2)}) async-start(), calls=%async_computation.13 | async-start | bytes 2359296 | tf_op jit(solution)/shard_map/all_gather | solution.py:145
  7.9 169.6 %all-gather.22.cloned.1.call-start = ((), (), s32[]{:S(2)}) async-start(), calls=%async_computation.18 | async-start | bytes 5242880 | tf_op jit(solution)/shard_map/all_gather | solution.py:191
  8.7 222.6 %all-gather.10.cloned.1.call-start = ((), (), s32[]{:S(2)}) async-start(), calls=%async_computation.11 | async-start | bytes 5242880 | tf_op jit(solution)/shard_map/all_gather | solution.py:160
  152.5 126.2 %all-gather.12.cloned.1.call-start = ((), (), s32[]{:S(2)}) async-start(), calls=%async_computation.12 | async-start | bytes 7077888 | tf_op jit(solution)/shard_map/all_gather | solution.py:143
  153.8 252.2 %all-gather.16.cloned.1.call-start = ((), (), s32[]{:S(2)}) async-start(), calls=%async_computation.14 | async-start | bytes 5242880 | tf_op jit(solution)/shard_map/all_gather | solution.py:161
  154.4 261.6 %all-gather.18.cloned.1.call-start = ((), (), s32[]{:S(2)}) async-start(), calls=%async_computation.15 | async-start | bytes 9437184 | tf_op jit(solution)/shard_map/all_gather | solution.py:146
  155.0 318.8 %all-gather.20.cloned.1.call-start = ((), (), s32[]{:S(2)}) async-start(), calls=%async_computation.16 | async-start | bytes 9437184 | tf_op jit(solution)/shard_map/all_gather | solution.py:148
  155.7 400.8 %reduce-scatter.24.cloned.1.call-start = ((), (), s32[]{:S(2)}) async-start(), calls=%async_computation.20 | async-start | bytes 5242880 | tf_op jit(solution)/shard_map/reduce_scatter | solution.py:239
  405.9 226.6 %reduce-scatter.22.cloned.1.call-start = ((), (), s32[]{:S(2)}) async-start(), calls=%async_computation.19 | async-start | bytes 5242880 | tf_op jit(solution)/shard_map/reduce_scatter | solution.py:242
  519.7 260.2 %reduce-scatter.20.cloned.1.call-start = ((), (), s32[]{:S(2)}) async-start(), calls=%async_computation.17 | async-start | bytes 10485760 | tf_op jit(solution)/shard_map/reduce_scatter | solution.py:184
  550.7 84.6 %copy-start.39 = (f32[256]{0:T(256)S(1)}, f32[256]{0:T(256)}, u32[]{:S(2)}) copy-start(f32[256]{0:T(256)} %copy-done.38) | copy-start | bytes 3076
  550.7 287.1 %reduce-scatter.34.cloned.1.call-start = ((), (), s32[]{:S(2)}) async-start(), calls=%async_computation.25 | async-start | bytes 147456
  555.0 301.0 %reduce-scatter.36.cloned.1.call-start = ((), (), s32[]{:S(2)}) async-start(), calls=%async_computation.26 | async-start | bytes 1179648
  556.5 223.4 %copy-start.36 = (f32[1,2048]{1,0:T(1,128)S(1)}, f32[1,2048]{1,0:T(1,128)}, u32[]{:S(2)}) copy-start(f32[1,2048]{1,0:T(1,128)} %get-tuple-element.328) | copy-start | bytes 24580
  556.5 223.4 %copy-start.37 = (f32[1,2048]{1,0:T(1,128)S(1)}, f32[1,2048]{1,0:T(1,128)}, u32[]{:S(2)}) copy-start(f32[1,2048]{1,0:T(1,128)} %get-tuple-element.329) | copy-start | bytes 24580
  556.5 439.3 %reduce-scatter.38.cloned.1.call-start = ((), (), s32[]{:S(2)}) async-start(), calls=%async_computation.27 | async-start | bytes 1081344
  556.6 223.3 %copy-start.4 = (bf16[256,2048]{1,0:T(8,128)(2,1)S(1)}, bf16[256,2048]{1,0:T(8,128)(2,1)}, u32[]{:S(2)}) copy-start(bf16[256,2048]{1,0:T(8,128)(2,1)} %reduce-scatter.24.cloned.1.call-done) | copy-start | bytes 3145732
  640.1 491.4 %reduce-scatter.40.cloned.1.call-start = ((), (), s32[]{:S(2)}) async-start(), calls=%async_computation.28 | async-start | bytes 1081344
  786.3 396.4 %reduce-scatter.28.cloned.1.call-start = ((), (), s32[]{:S(2)}) async-start(), calls=%async_computation.22 | async-start | bytes 4718592 | tf_op jit(solution)/shard_map/reduce_scatter | solution.py:258
  793.2 485.6 %reduce-scatter.26.cloned.1.call-start = ((), (), s32[]{:S(2)}) async-start(), calls=%async_computation.21 | async-start | bytes 14155776 | tf_op jit(solution)/shard_map/reduce_scatter | solution.py:256
  806.7 592.1 %reduce-scatter.32.cloned.1.call-start = ((), (), s32[]{:S(2)}) async-start(), calls=%async_computation.24 | async-start | bytes 18874368 | tf_op jit(solution)/shard_map/reduce_scatter | solution.py:261
  822.1 696.9 %reduce-scatter.30.cloned.1.call-start = ((), (), s32[]{:S(2)}) async-start(), calls=%async_computation.23 | async-start | bytes 18874368 | tf_op jit(solution)/shard_map/reduce_scatter | solution.py:259
  (49 other events, 689.5 us)
Sparse Core Ops, SparseCore 0:
  9.9 30.8 all-gather.13
  42.3 81.0 all-gather.21
  152.7 78.5 all-gather.9
  233.6 45.0 all-gather.11
  280.7 80.7 all-gather.15
  363.2 52.7 all-gather.17
  417.9 55.8 all-gather.19
  476.0 76.7 reduce-scatter.23
  555.2 77.2 reduce-scatter.21
  634.7 145.1 reduce-scatter.19
  782.9 34.1 reduce-scatter.33
  820.1 35.9 reduce-scatter.35
  858.3 137.3 reduce-scatter.37
  997.9 133.5 reduce-scatter.39
  1135.3 47.4 reduce-scatter.27
  1186.7 92.0 reduce-scatter.25
  1282.8 115.9 reduce-scatter.31
  1402.8 116.1 reduce-scatter.29
where the time goes:
time: 1530 us
  waiting for transfers between devices  1040 us (68%)
  matrix products  177 us (12%)
  blocking collectives  155 us (10%)
  local copies, waits for them, and re-layouts  69 us (5%)
  other arithmetic  58 us (4%)
    unnamed x22, waiting for transfers between devices  293 us
    reduce_scatter x1, waiting for transfers between devices, shards(): lax.psum_scatter(attn_part + jnp.dot(activated, back_weight, preferred_el...  140 us
    reduce_scatter x1, waiting for transfers between devices, shards(): lax.psum_scatter(up_term, 'dp', scatter_dimension=0, tiled=True)  120 us
    reduce_scatter x1, waiting for transfers between devices, shards(): lax.psum_scatter(down_term, 'dp', scatter_dimension=1, tiled=True)  120 us
    reduce_scatter x1, waiting for transfers between devices, shards(): lax.psum_scatter(joined_term, 'dp', scatter_dimension=0, tiled=True)  96 us
    reduce_scatter x1, waiting for transfers between devices, shards(): lax.psum_scatter(grad_second.astype(jnp.bfloat16), 'tensor', scatter_dime...  75.9 us
    all_gather x1, blocking collectives, shards(): lax.all_gather(norm_gains, ('dp', 'tensor'), axis=1, tiled=True)  71.2 us
    all_gather x1, blocking collectives, shards(): lax.all_gather(biases, ('dp', 'tensor'), axis=1, tiled=True)  66 us
  transfers between devices with their start and end apart: 18, of which 13 were waited for; matrix products, arithmetic and copies ran while one was open for 19% of the time, Pallas kernels for 0%

commit v1 on v0

--- a/solution.py
+++ b/solution.py
@@ -6,6 +6,27 @@
 ROT = 64
 EPSILON = 1e-05
 ROTARY_BASE = 10000.0
+
+
+def ring_gather(array, axis, dim):
+    size, position, rows = (lax.axis_size(axis), lax.axis_index(axis), array.shape[dim])
+    right = [(i, (i + 1) % size) for i in range(size)]
+    left = [(i, (i - 1) % size) for i in range(size)]
+    filled = jnp.zeros((*array.shape[:dim], size * rows, *array.shape[dim + 1 :]), array.dtype)
+    filled = lax.dynamic_update_slice_in_dim(filled, array, position * rows, axis=dim)
+    from_left = from_right = array
+    half = size // 2
+    for hop in range(1, half + 1):
+        from_left = lax.ppermute(from_left, axis, right)
+        filled = lax.dynamic_update_slice_in_dim(
+            filled, from_left, (position - hop) % size * rows, axis=dim
+        )
+        if hop < size - half:
+            from_right = lax.ppermute(from_right, axis, left)
+            filled = lax.dynamic_update_slice_in_dim(
+                filled, from_right, (position + hop) % size * rows, axis=dim
+            )
+    return filled
 
 
 def layer_norm(values, gain_row, shift_row):
@@ -140,7 +161,7 @@
     block_rows = min(512, row_count)
     dp_index = lax.axis_index("dp")
     gathered = (
-        lax.all_gather(proj_weight, "dp", axis=0, tiled=True),
+        ring_gather(proj_weight, "dp", 0),
         lax.all_gather(proj_bias, "dp", axis=2, tiled=True),
         lax.all_gather(out_weight, "dp", axis=1, tiled=True),
         lax.all_gather(up_weight, "dp", axis=0, tiled=True),

time: 1530 us -> 1640 us (1.072)
  waiting for transfers between devices: 1040 us -> 1120 us
    all_gather x1, waiting for transfers between devices: 0.01 us -> 73.4 us  [shards(): grad_rows = lax.all_gather(cotangent, 'tensor', axis=0, tiled=True)]
    all_gather x1, waiting for transfers between devices: 47.5 us -> 0.01 us  [shards(): lax.all_gather(first_local.astype(jnp.bfloat16), 'tensor', axis=0, tiled=...]
    all_gather x1, waiting for transfers between devices: 47.4 us -> 0.02 us  [shards(): lax.all_gather(proj_weight, 'dp', axis=0, tiled=True)]
    all_gather x1, waiting for transfers between devices: 10 us -> 54.5 us  [shards(): lax.all_gather(up_weight, 'dp', axis=0, tiled=True)]
    all_gather x1, waiting for transfers between devices: 0.02 us -> 32.5 us  [shards(): lax.all_gather(second_local.astype(jnp.bfloat16), 'tensor', axis=0, tiled...]
    ppermute x0 -> x7, waiting for transfers between devices: none -> 17.4 us  [the longest x4 17 us: ring_gather(): from_left = lax.ppermute(from_left, axis, right)]
    unnamed x94 -> x96, local copies, waits for them, and re-layouts: 34.8 us -> 25.5 us
  transfers between devices with their start and end apart: 18 -> 25, of which waited for: 13 -> 16; matrix products, arithmetic and copies ran while one was open for 19% -> 18% of each run, Pallas kernels for 0% -> 0%
where the time goes in v1:
time: 1640 us; the launch traced here: 1630 us
  waiting for transfers between devices  1120 us (68%)
  matrix products  190 us (12%)
  blocking collectives  170 us (10%)
  local copies, waits for them, and re-layouts  69.5 us (4%)
  other arithmetic  56.5 us (3%)
    unnamed x22, waiting for transfers between devices  293 us
    reduce_scatter x1, waiting for transfers between devices, shards(): lax.psum_scatter(attn_part + jnp.dot(activated, back_weight, preferred_el...  140 us
    reduce_scatter x1, waiting for transfers between devices, shards(): lax.psum_scatter(up_term, 'dp', scatter_dimension=0, tiled=True)  120 us
    reduce_scatter x1, waiting for transfers between devices, shards(): lax.psum_scatter(down_term, 'dp', scatter_dimension=1, tiled=True)  120 us
    reduce_scatter x1, waiting for transfers between devices, shards(): lax.psum_scatter(joined_term, 'dp', scatter_dimension=0, tiled=True)  96 us
    reduce_scatter x1, waiting for transfers between devices, shards(): lax.psum_scatter(grad_second.astype(jnp.bfloat16), 'tensor', scatter_dime...  75.7 us
    all_gather x1, waiting for transfers between devices, shards(): grad_rows = lax.all_gather(cotangent, 'tensor', axis=0, tiled=True)  73.4 us
    all_gather x1, blocking collectives, shards(): lax.all_gather(norm_gains, ('dp', 'tensor'), axis=1, tiled=True)  70 us
  transfers between devices with their start and end apart: 25, of which 16 were waited for; matrix products, arithmetic and copies ran while one was open for 18% of the time, Pallas kernels for 0%

profile of v1, /device:TPU:0, one launch (start us, length us, event | category | flops | bytes accessed | tf_op | source)
XLA Modules:
  0.0 1631.3 jit_solution(13693049485644384767)
XLA Ops:
  10.4 70.0 %all-gather = bf16[32,64,2]{1,2,0:T(2,128)(2,1)S(1)} all-gather(bf16[1,64,2]{1,2,0:T(2,128)(2,1)} %bitcast.182), channel_id=1, replica_groups=mesh['dp'=8,'tensor'=4] {'dp','tensor'}, dimensions={0}, use_global_device_ids=true | all-gather | bytes 8448 | tf_op jit(solution)/shard_map/all_gather | solution.py:173
  80.5 63.8 %all-gather.1 = bf16[32,64,4]{1,2,0:T(4,128)(2,1)S(1)} all-gather(bf16[1,64,4]{1,2,0:T(4,128)(2,1)} %bitcast.181), channel_id=1, replica_groups=mesh['dp'=8,'tensor'=4] {'dp','tensor'}, dimensions={0}, use_global_device_ids=true | all-gather | bytes 16896 | tf_op jit(solution)/shard_map/all_gather | solution.py:174
  167.3 15.3 all_gather.39
  184.5 21.1 %all_gather.43 = bf16[1,2048]{1,0:T(2,128)(2,1)S(1)} all-gather(bf16[1,256]{1,0:T(2,128)(2,1)S(1)} %copy-done.45), channel_id=1, replica_groups=mesh['dp'=8,'tensor'=4] {'dp'}, dimensions={1}, use_global_device_ids=true | all-gather | bytes 4608 | tf_op jit(solution)/shard_map/all_gather | solution.py:168
  264.7 73.4 %all-gather.20.cloned.1.call-done = bf16[1024,2048]{1,0:T(8,128)(2,1)} async-done(((bf16[256,2048]{1,0:T(8,128)(2,1)}), bf16[1024,2048]{1,0:T(8,128)(2,1)}) %all-gather.20.cloned.1.call-update) | async-done | bytes 4194320 | tf_op jit(solution)/shard_map/all_gather | solution.py:212
  344.4 19.1 %while.27 = (s32[]{:T(128)}, bf16[2,512,2,256]{3,1,2,0:T(8,128)(2,1)}, f32[2,2,512]{2,1,0:T(2,128)S(1)}, s32[2]{0:T(128)S(1)}, s32[1024]{0:T(1024)S(1)}, /*index...) while((s32[]{:T(128)}, ...), condition=%wide.region_5.6_spmd, body=%wide.region_2.0_spmd.sunk | while | flops 1087897088 | bytes 18397868 | solution.py:99
  363.5 40.1 %while.28 = (s32[]{:T(128)}, f32[1024,2,256]{0,2,1:T(8,128)}, f32[1024,2,256]{0,2,1:T(8,128)}, f32[2,512,2,256]{3,1,0,2:T(8,128)}, s32[2]{0:T(128)S(1)}, /*index...) while((s32[]{:T(128)}, f32[1024,2,256]{0,2,1:T(8,128)}, ...), condition=%wide.region_12.13_spmd.clone, body=%wide.region_10.12_spmd.clone.sunk | while | flops 2704539136 | bytes 123775488 | solution.py:140
  434.0 32.5 %all-gather.14.cloned.1.call-done = bf16[1024,2048]{1,0:T(8,128)(2,1)} async-done(((bf16[256,2048]{1,0:T(8,128)(2,1)}), bf16[1024,2048]{1,0:T(8,128)(2,1)}) %all-gather.14.cloned.1.call-update) | async-done | bytes 4194320 | tf_op jit(solution)/shard_map/all_gather | solution.py:182
  466.6 54.5 %all-gather.16.cloned.1.call-done = bf16[2048,2048]{1,0:T(8,128)(2,1)} async-done(((bf16[256,2048]{1,0:T(8,128)(2,1)}), bf16[2048,2048]{1,0:T(8,128)(2,1)}) %all-gather.16.cloned.1.call-update) | async-done | bytes 8388624 | tf_op jit(solution)/shard_map/all_gather | solution.py:167
  521.1 14.7 fusion.78
  535.8 43.1 %all-gather.18.cloned.1.call-done = bf16[2048,2048]{1,0:T(8,128)(2,1)} async-done(((bf16[2048,256]{1,0:T(8,128)(2,1)}), bf16[2048,2048]{1,0:T(8,128)(2,1)}) %all-gather.18.cloned.1.call-update) | async-done | bytes 8388624 | tf_op jit(solution)/shard_map/all_gather | solution.py:169
  578.9 33.1 %convert_reduce_fusion = (f32[2048]{0:T(1024)S(1)}, bf16[1024,2048]{1,0:T(8,128)(2,1)S(1)}, f32[1024,2048]{1,0:T(8,128)}) fusion(f32[1024,2048]{1,0:T(8,128)} %fusion.78, f32[2048]{0:T(1024)S(1)} %bitcast.166, bf16[1024,2048]{1,0:T(8,128)(2,1)} %all-gather.20.cloned.1.call-done, bf16[2048,2048]{1,0:T(8,128)(2,1)} %all-gather.18.cloned.1.call-done), kind=kOutput, calls=%fused_computation.50 | convolution fusion | flops 8747218944 | bytes 33570816 | tf_op jit(solution)/shard_map/nd,fd->nf/dot_general | solution.py:222
  637.4 12.7 fusion.79
  661.9 75.7 %reduce-scatter.22.cloned.1.call-done = bf16[256,2048]{1,0:T(8,128)(2,1)} async-done(((bf16[1024,2048]{1,0:T(8,128)(2,1)}), bf16[256,2048]{1,0:T(8,128)(2,1)}) %reduce-scatter.22.cloned.1.call-update) | async-done | bytes 1048592 | tf_op jit(solution)/shard_map/reduce_scatter | solution.py:263
  745.2 139.7 %reduce-scatter.20.cloned.1.call-done = f32[256,2048]{1,0:T(8,128)} async-done(((f32[1024,2048]{1,0:T(8,128)}), f32[256,2048]{1,0:T(8,128)}) %reduce-scatter.20.cloned.1.call-update) | async-done | bytes 2097168 | tf_op jit(solution)/shard_map/reduce_scatter | solution.py:205
  911.8 15.2 fusion.82
  927.4 15.2 fusion.81
  944.1 17.1 %reduce-scatter.36.cloned.1.call-done = f32[256,1]{1,0:T(8,128)} async-done(((f32[2048,1]{1,0:T(8,128)}), f32[256,1]{1,0:T(8,128)}) %reduce-scatter.36.cloned.1.call-update) | async-done | bytes 1040
  962.7 138.1 %reduce-scatter.38.cloned.1.call-done = f32[64,2]{1,0:T(8,128)} async-done(((f32[2048,2]{1,0:T(8,128)}), f32[64,2]{1,0:T(8,128)}) %reduce-scatter.38.cloned.1.call-update) | async-done | bytes 528
  1102.3 134.6 %reduce-scatter.40.cloned.1.call-done = f32[64,4]{1,0:T(8,128)} async-done(((f32[2048,4]{1,0:T(8,128)}), f32[64,4]{1,0:T(8,128)}) %reduce-scatter.40.cloned.1.call-update) | async-done | bytes 1040
  1238.3 49.7 %reduce-scatter.28.cloned.1.call-done = f32[512,256]{1,0:T(8,128)} async-done(((f32[512,2048]{1,0:T(8,128)}), f32[512,256]{1,0:T(8,128)}) %reduce-scatter.28.cloned.1.call-update) | async-done | bytes 524304 | tf_op jit(solution)/shard_map/reduce_scatter | solution.py:279
  1288.0 96.0 %reduce-scatter.26.cloned.1.call-done = f32[256,3,512]{2,0,1:T(8,128)} async-done(((f32[2048,3,512]{2,0,1:T(8,128)}), f32[256,3,512]{2,0,1:T(8,128)}) %reduce-scatter.26.cloned.1.call-update) | async-done | bytes 1572880 | tf_op jit(solution)/shard_map/reduce_scatter | solution.py:277
  1384.0 120.0 %reduce-scatter.32.cloned.1.call-done = f32[2048,256]{1,0:T(8,128)} async-done(((f32[2048,2048]{1,0:T(8,128)}), f32[2048,256]{1,0:T(8,128)}) %reduce-scatter.32.cloned.1.call-update) | async-done | bytes 2097168 | tf_op jit(solution)/shard_map/reduce_scatter | solution.py:282
  1504.0 120.2 %reduce-scatter.30.cloned.1.call-done = f32[256,2048]{1,0:T(8,128)} async-done(((f32[2048,2048]{1,0:T(8,128)}), f32[256,2048]{1,0:T(8,128)}) %reduce-scatter.30.cloned.1.call-update) | async-done | bytes 2097168 | tf_op jit(solution)/shard_map/reduce_scatter | solution.py:280
  (311 shorter events, 252.5 us)
Async XLA Ops:
  7.2 227.6 %all-gather.10.cloned.1.call-start = ((), (), s32[]{:S(2)}) async-start(), calls=%async_computation.11 | async-start | bytes 5242880 | tf_op jit(solution)/shard_map/all_gather | solution.py:181
  148.4 116.3 %all-gather.12.cloned.1.call-start = ((), (), s32[]{:S(2)}) async-start(), calls=%async_computation.12 | async-start | bytes 2359296 | tf_op jit(solution)/shard_map/all_gather | solution.py:166
  149.2 189.0 %all-gather.20.cloned.1.call-start = ((), (), s32[]{:S(2)}) async-start(), calls=%async_computation.17 | async-start | bytes 5242880 | tf_op jit(solution)/shard_map/all_gather | solution.py:212
  149.9 272.6 %all-gather.22.cloned.1.call-start = ((), (), s32[]{:S(2)}) async-start(), calls=%async_computation.19 | async-start | bytes 7077888 | tf_op jit(solution)/shard_map/all_gather | solution.py:214
  150.5 316.1 %all-gather.14.cloned.1.call-start = ((), (), s32[]{:S(2)}) async-start(), calls=%async_computation.13 | async-start | bytes 5242880 | tf_op jit(solution)/shard_map/all_gather | solution.py:182
  151.1 370.0 %all-gather.16.cloned.1.call-start = ((), (), s32[]{:S(2)}) async-start(), calls=%async_computation.14 | async-start | bytes 9437184 | tf_op jit(solution)/shard_map/all_gather | solution.py:167
  151.7 427.2 %all-gather.18.cloned.1.call-start = ((), (), s32[]{:S(2)}) async-start(), calls=%async_computation.15 | async-start | bytes 9437184 | tf_op jit(solution)/shard_map/all_gather | solution.py:169
  151.7 15.3 collective-permute-start
  151.8 30.9 %collective-permute-start.1 = (bf16[256,3,512]{2,0,1:T(8,128)(2,1)S(1)}, bf16[256,3,512]{2,0,1:T(8,128)(2,1)S(1)}, u32[]{:S(2)}, u32[]{:S(2)}) collective-permute-start(bf16[256,3,512]{2,0,1:T(8,128)(2,1)S(1)} %copy-done.24), channel_id=1, source_target_pairs={{0,28},{4,0},{8,4},{12,8},{16,12},{20,16},{24,20},{28,24},{1,29},{... | collective-permute-start | bytes 2359304 | tf_op jit(solution)/shard_map/ppermute | solution.py:25
  167.1 16.9 %collective-permute-start.2 = (bf16[256,3,512]{2,0,1:T(8,128)(2,1)S(1)}, bf16[256,3,512]{2,0,1:T(8,128)(2,1)S(1)}, u32[]{:S(2)}, u32[]{:S(2)}) collective-permute-start(bf16[256,3,512]{2,0,1:T(8,128)(2,1)S(1)} %collective-permute-done), channel_id=1, source_target_pairs={{0,4},{4,8},{8,12},{12,16},{16,20},{20,24},{24,28},{28,0},{1,5},{5... | collective-permute-start | bytes 2359304 | tf_op jit(solution)/shard_map/ppermute | solution.py:20
  167.1 494.8 %reduce-scatter.24.cloned.1.call-start = ((), (), s32[]{:S(2)}) async-start(), calls=%async_computation.20 | async-start | bytes 5242880 | tf_op jit(solution)/shard_map/reduce_scatter | solution.py:260
  182.6 28.0 %collective-permute-start.3 = (bf16[256,3,512]{2,0,1:T(8,128)(2,1)S(1)}, bf16[256,3,512]{2,0,1:T(8,128)(2,1)}, u32[]{:S(2)}, u32[]{:S(2)}) collective-permute-start(bf16[256,3,512]{2,0,1:T(8,128)(2,1)S(1)} %collective-permute-done.1), channel_id=1, source_target_pairs={{0,28},{4,0},{8,4},{12,8},{16,12},{20,16},{24,20},{28,24},{1,29},{... | collective-permute-start | bytes 2359304 | tf_op jit(solution)/shard_map/ppermute | solution.py:25
  184.0 32.6 %collective-permute-start.4 = (bf16[256,3,512]{2,0,1:T(8,128)(2,1)S(1)}, bf16[256,3,512]{2,0,1:T(8,128)(2,1)}, u32[]{:S(2)}, u32[]{:S(2)}) collective-permute-start(bf16[256,3,512]{2,0,1:T(8,128)(2,1)S(1)} %collective-permute-done.2), channel_id=1, source_target_pairs={{0,4},{4,8},{8,12},{12,16},{16,20},{20,24},{24,28},{28,0},{1,5},{5... | collective-permute-start | bytes 2359304 | tf_op jit(solution)/shard_map/ppermute | solution.py:20
  216.6 15.8 collective-permute-start.6
  434.0 303.6 %reduce-scatter.22.cloned.1.call-start = ((), (), s32[]{:S(2)}) async-start(), calls=%async_computation.18 | async-start | bytes 5242880 | tf_op jit(solution)/shard_map/reduce_scatter | solution.py:263
  624.8 260.1 %reduce-scatter.20.cloned.1.call-start = ((), (), s32[]{:S(2)}) async-start(), calls=%async_computation.16 | async-start | bytes 10485760 | tf_op jit(solution)/shard_map/reduce_scatter | solution.py:205
  655.9 286.7 %reduce-scatter.34.cloned.1.call-start = ((), (), s32[]{:S(2)}) async-start(), calls=%async_computation.25 | async-start | bytes 147456
  660.3 300.9 %reduce-scatter.36.cloned.1.call-start = ((), (), s32[]{:S(2)}) async-start(), calls=%async_computation.26 | async-start | bytes 1179648
  661.8 439.1 %reduce-scatter.38.cloned.1.call-start = ((), (), s32[]{:S(2)}) async-start(), calls=%async_computation.27 | async-start | bytes 1081344
  745.2 491.7 %reduce-scatter.40.cloned.1.call-start = ((), (), s32[]{:S(2)}) async-start(), calls=%async_computation.28 | async-start | bytes 1081344
  891.4 396.6 %reduce-scatter.28.cloned.1.call-start = ((), (), s32[]{:S(2)}) async-start(), calls=%async_computation.22 | async-start | bytes 4718592 | tf_op jit(solution)/shard_map/reduce_scatter | solution.py:279
  898.2 485.8 %reduce-scatter.26.cloned.1.call-start = ((), (), s32[]{:S(2)}) async-start(), calls=%async_computation.21 | async-start | bytes 14155776 | tf_op jit(solution)/shard_map/reduce_scatter | solution.py:277
  911.8 592.3 %reduce-scatter.32.cloned.1.call-start = ((), (), s32[]{:S(2)}) async-start(), calls=%async_computation.24 | async-start | bytes 18874368 | tf_op jit(solution)/shard_map/reduce_scatter | solution.py:282
  927.1 697.2 %reduce-scatter.30.cloned.1.call-start = ((), (), s32[]{:S(2)}) async-start(), calls=%async_computation.23 | async-start | bytes 18874368 | tf_op jit(solution)/shard_map/reduce_scatter | solution.py:280
  (59 other events, 2176.7 us)
Sparse Core Ops, SparseCore 0:
  148.5 78.6 all-gather.9
  229.1 26.5 all-gather.11
  257.3 80.7 all-gather.19
  339.9 43.8 all-gather.21
  385.8 80.7 all-gather.13
  468.3 52.7 all-gather.15
  523.0 55.8 all-gather.17
  581.1 76.7 reduce-scatter.23
  660.3 77.2 reduce-scatter.21
  739.8 145.1 reduce-scatter.19
  887.9 34.1 reduce-scatter.33
  925.2 35.9 reduce-scatter.35
  963.4 137.3 reduce-scatter.37
  1103.0 133.8 reduce-scatter.39
  1240.7 47.2 reduce-scatter.27
  1291.9 92.0 reduce-scatter.25
  1388.0 115.9 reduce-scatter.31
  1508.0 116.1 reduce-scatter.29
